TPU v7x, 128 devices: a whole 4x4x4 slice. The times are simulated.
128 devices in a mesh: req: 32 (over x, z, core), tp: 4 (over y).
Axes of the slice: x: 4, y: 4, z: 4, core: 2. Of those that a mesh axis runs over, the one named last changes fastest.
Arguments:
- hidden_states: bfloat16 [8192, 2048], P('req'), may hold values from -30 to 30
- norm_gain: float32 [2048], replicated, may hold values from 0.5 to 1.5
- head: bfloat16 [2048, 98304], P(None, ('req', 'tp')), may hold values from -1 to 1
- target_ids: int32 [8192], P('req'), may hold values from 0 to 98303
- lengths: int32 [32], P('req'), may hold values from 32 to 256, as said below
Outputs:
- token_logprob: float32 [8192], P('req')
- token_entropy: float32 [8192], P('req')
- seq_mean_logprob: float32 [32], P('req')
- seq_top_logit: float32 [32], P('req')
Inputs may be any that keep to these rules, and one draw needn't show every extreme that they name: `lengths`: each completion has at least 32 and at most 256 live slots; some completion has exactly 256.
All inputs are finite; a program needn't handle non-finite values.
Results may differ from a plain program's by a relative error of at most 0.0018.
Values may be sent and summed in bfloat16 or wider, within the bound.
A program may use at most 128 MiB of HBM per device.

v0:
```python
import jax
import jax.numpy as jnp
from jax import lax
from jax.sharding import PartitionSpec as P

CHUNKS = 4


def chunk_stats(block, target, matrix, vocab_ids):
    logits = jnp.dot(block, matrix, preferred_element_type=jnp.float32)
    top = jnp.max(logits, axis=-1)
    shifted = jnp.exp(logits - top[:, None])
    weight_sum = jnp.sum(shifted, axis=-1)
    weighted = jnp.sum(shifted * logits, axis=-1)
    hit = vocab_ids == target[:, None]
    picked = jnp.sum(jnp.where(hit, logits, 0.0), axis=-1)
    return jnp.stack([top, weight_sum, weighted, picked])


def merge(stats, axis):
    top = jnp.max(stats[:, 0], axis=axis)
    factor = jnp.exp(stats[:, 0] - jnp.expand_dims(top, axis))
    return (
        top,
        jnp.sum(stats[:, 1] * factor, axis=axis),
        jnp.sum(stats[:, 2] * factor, axis=axis),
        jnp.sum(stats[:, 3], axis=axis),
    )


def per_device(hidden_states, norm_gain, head, target_ids, lengths):
    feats = hidden_states.astype(jnp.float32)
    scale = lax.rsqrt(jnp.mean(feats * feats, axis=-1, keepdims=True) + 1e-06)
    normed = (feats * scale * norm_gain).astype(jnp.bfloat16)
    rows = hidden_states.shape[0]
    vdev = head.shape[1]
    n_req = lax.axis_size("req")
    n_tp = lax.axis_size("tp")
    vbase = (lax.axis_index("req") * n_tp + lax.axis_index("tp")) * vdev
    own_vocab = lax.broadcasted_iota(jnp.int32, (1, vdev), 1) + vbase
    step = rows // CHUNKS
    digits = jnp.concatenate([target_ids % 64, target_ids // 64 % 64, target_ids // 4096])
    extra = jnp.zeros((16, normed.shape[1]), jnp.bfloat16)
    extra = extra.at[0, : 3 * rows].set(digits.astype(jnp.bfloat16))
    parts = []
    targets = None
    for c in range(CHUNKS):
        piece = normed[c * step : (c + 1) * step]
        if c == 0:
            piece = jnp.concatenate([piece, extra], axis=0)
        block = lax.all_gather(piece, "req", axis=0, tiled=False)
        if c == 0:
            code = block[:, step, : 3 * rows].astype(jnp.int32).reshape(n_req, 3, rows)
            targets = code[:, 0] + code[:, 1] * 64 + code[:, 2] * 4096
            block = block[:, :step]
        target = targets[:, c * step : (c + 1) * step].reshape(-1)
        st = chunk_stats(block.reshape(-1, block.shape[2]), target, head, own_vocab)
        parts.append(st.reshape(4, n_req, step))
    stats = jnp.concatenate(parts, axis=2)
    arrived = lax.all_to_all(stats, "req", split_axis=1, concat_axis=1, tiled=True)
    own = merge(jnp.moveaxis(arrived, 1, 0), axis=0)
    own = jnp.stack(own)
    everyone = lax.all_gather(own, "tp", axis=0)
    top, weight_sum, weighted, picked = merge(everyone, axis=0)
    log_norm = top + jnp.log(weight_sum)
    live = jnp.arange(rows, dtype=jnp.int32) < lengths[0]
    logprob = jnp.where(live, picked - log_norm, jnp.float32(0.0))
    entropy = jnp.where(live, log_norm - weighted / weight_sum, jnp.float32(0.0))
    mean_lp = (jnp.sum(logprob) / lengths[0].astype(jnp.float32)).reshape(1)
    top_live = jnp.max(jnp.where(live, top, jnp.float32(-1e30))).reshape(1)
    return (logprob, entropy, mean_lp, top_live)


def solution(mesh):
    in_specs = (P("req", None), P(), P(None, ("req", "tp")), P("req"), P("req"))
    out_specs = (P("req"), P("req"), P("req"), P("req"))
    return jax.shard_map(
        per_device, mesh=mesh, in_specs=in_specs, out_specs=out_specs, check_vma=False
    )
```

profile of v0, /device:TPU:0, one launch (start us, length us, event | category | flops | bytes accessed | tf_op | source)
XLA Modules:
  0.0 306.7 jit_solution(13360459740497236305)
XLA Ops:
  7.2 1.7 fusion.4
  8.9 1.5 fusion.6
  10.4 0.9 fusion.33
  11.4 0.7 all-gather.15.cloned.1.call-update
  12.2 0.7 all-gather.17.cloned.1.call-update
  12.9 0.7 fusion.29
  13.7 0.8 pad_maximum_fusion
  14.5 52.5 %all-gather.13.cloned.1.call-done = bf16[2048,2048]{1,0:T(8,128)(2,1)} async-done(((bf16[64,2048]{1,0:T(8,128)(2,1)}), bf16[2048,2048]{1,0:T(8,128)(2,1)}) %all-gather.13.cloned.1.call-update) | async-done | bytes 8388624 | tf_op jit(solution)/shard_map/all_gather | solution.py:51
  67.0 10.8 %fusion.38 = (f32[2048]{0:T(1024)S(1)}, f32[2048,768]{0,1:T(8,128)}) fusion(bf16[2048,2048]{1,0:T(8,128)(2,1)} %all-gather.13.cloned.1.call-done, bf16[2048,768]{1,0:T(8,128)(2,1)S(1)} %copy-done), kind=kOutput, calls=%fused_computation.92 | convolution fusion | flops 6444021760 | bytes 17833984 | tf_op jit(solution)/shard_map/dot_general | solution.py:10
  77.8 0.1 stack.80
  77.9 43.9 %all-gather.15.cloned.1.call-done = bf16[2048,2048]{1,0:T(8,128)(2,1)} async-done(((bf16[64,2048]{1,0:T(8,128)(2,1)}), bf16[2048,2048]{1,0:T(8,128)(2,1)}) %all-gather.15.cloned.1.call-update) | async-done | bytes 8388624 | tf_op jit(solution)/shard_map/all_gather | solution.py:51
  121.8 10.8 %fusion.39 = (f32[2048]{0:T(1024)S(1)}, f32[2048,768]{0,1:T(8,128)}) fusion(bf16[2048,2048]{1,0:T(8,128)(2,1)} %all-gather.15.cloned.1.call-done, bf16[2048,768]{1,0:T(8,128)(2,1)S(1)} %copy-done), kind=kOutput, calls=%fused_computation.93 | convolution fusion | flops 6444021760 | bytes 17833984 | tf_op jit(solution)/shard_map/dot_general | solution.py:10
  132.6 0.1 stack.85
  132.7 44.0 %all-gather.17.cloned.1.call-done = bf16[2048,2048]{1,0:T(8,128)(2,1)} async-done(((bf16[64,2048]{1,0:T(8,128)(2,1)}), bf16[2048,2048]{1,0:T(8,128)(2,1)}) %all-gather.17.cloned.1.call-update) | async-done | bytes 8388624 | tf_op jit(solution)/shard_map/all_gather | solution.py:51
  176.7 10.8 %fusion.40 = (f32[2048]{0:T(1024)S(1)}, f32[2048,768]{0,1:T(8,128)}) fusion(bf16[2048,2048]{1,0:T(8,128)(2,1)} %all-gather.17.cloned.1.call-done, bf16[2048,768]{1,0:T(8,128)(2,1)S(1)} %copy-done), kind=kOutput, calls=%fused_computation.94 | convolution fusion | flops 6444021760 | bytes 17833984 | tf_op jit(solution)/shard_map/dot_general | solution.py:10
  187.4 0.1 stack.90
  187.5 48.7 %all-gather.11.cloned.1.call-done = bf16[2560,2048]{1,0:T(8,128)(2,1)} async-done(((bf16[80,2048]{1,0:T(8,128)(2,1)}), bf16[2560,2048]{1,0:T(8,128)(2,1)}) %all-gather.11.cloned.1.call-update) | async-done | bytes 10485776 | tf_op jit(solution)/shard_map/all_gather | solution.py:51
  236.2 1.0 slice.104
  237.3 8.4 %slice.103 = bf16[32,64,2048]{2,1,0:T(8,128)(2,1)} slice(bf16[32,80,2048]{2,1,0:T(8,128)(2,1)} %bitcast.69), slice={[0:32], [0:64], [0:2048]} | slice | bytes 16777216 | tf_op jit(solution)/shard_map/slice | solution.py:55
  246.2 10.9 %fusion.37 = (f32[2048]{0:T(1024)S(1)}, f32[2048,768]{0,1:T(8,128)}) fusion(bf16[2048,2048]{1,0:T(8,128)(2,1)} %bitcast.67, bf16[2048,768]{1,0:T(8,128)(2,1)S(1)} %copy-done), kind=kOutput, calls=%fused_computation.91 | convolution fusion | flops 6444021760 | bytes 17833984 | tf_op jit(solution)/shard_map/dot_general | solution.py:10
  257.1 0.1 stack.75
  257.2 12.0 %fusion.3 = (f32[2048]{0:T(1024)S(1)}, f32[2048]{0:T(1024)S(1)}, f32[2048]{0:T(1024)S(1)}, f32[2048]{0:T(1024)S(1)}, f32[2048]{0:T(1024)S(1)}, /*index=5*/f32[20...) fusion(f32[2048,768]{0,1:T(8,128)} %get-tuple-element.71, ...), kind=kLoop, calls=%fused_computation.15 | loop fusion | flops 44015616 | bytes 25332736 | tf_op jit(solution)/shard_map/reduce_sum | solution.py:13
  269.2 0.1 stack.76
  269.5 0.1 stack.82
  269.7 0.1 stack.87
  270.0 0.1 stack.92
  270.1 1.1 maximum_maximum_fusion
  271.3 5.4 %all-to-all-start = ((f32[4,32,256]{2,0,1:T(4,128)}), f32[4,32,256]{2,0,1:T(4,128)S(1)}, u32[]{:S(2)}, u32[]{:S(2)}) async-start(f32[4,32,256]{2,0,1:T(4,128)} %maximum_maximum_fusion), calls=%async_computation | async-start | bytes 262144 | tf_op jit(solution)/shard_map/all_to_all | solution.py:60
  277.4 7.2 %all-to-all-done = f32[4,32,256]{2,0,1:T(4,128)S(1)} async-done(((f32[4,32,256]{2,0,1:T(4,128)}), f32[4,32,256]{2,0,1:T(4,128)S(1)}, u32[]{:S(2)}, u32[]{:S(2)}) %all-to-all-start) | async-done | bytes 131104 | tf_op jit(solution)/shard_map/all_to_all | solution.py:60
  284.6 0.1 fusion.34
  284.7 12.3 %all-gather.5 = f32[4,4,256]{2,1,0:T(4,128)S(1)} all-gather(f32[1,4,256]{2,1,0:T(4,128)S(1)} %maximum_bitcast_fusion), channel_id=6, replica_groups=mesh['req'=32,'tp'=4] {'tp'}, dimensions={0}, use_global_device_ids=true | all-gather | bytes 20480 | tf_op jit(solution)/shard_map/all_gather | solution.py:63
  297.1 1.3 fusion.32
  (35 shorter events, 1.5 us)
Async XLA Ops:
  7.2 59.9 %copy-start = (bf16[2048,768]{1,0:T(8,128)(2,1)S(1)}, bf16[2048,768]{1,0:T(8,128)(2,1)}, u32[]{:S(2)}) copy-start(bf16[2048,768]{1,0:T(8,128)(2,1)} %param.9) | copy-start | bytes 9437188
  7.2 59.9 %all-gather.13.cloned.1.call-start = ((), (), s32[]{:S(2)}) async-start(), calls=%async_computation.2 | async-start | bytes 8650752 | tf_op jit(solution)/shard_map/all_gather | solution.py:51
  11.4 110.5 %all-gather.15.cloned.1.call-start = ((), (), s32[]{:S(2)}) async-start(), calls=%async_computation.3 | async-start | bytes 8650752 | tf_op jit(solution)/shard_map/all_gather | solution.py:51
  12.1 164.5 %all-gather.17.cloned.1.call-start = ((), (), s32[]{:S(2)}) async-start(), calls=%async_computation.4 | async-start | bytes 8650752 | tf_op jit(solution)/shard_map/all_gather | solution.py:51
  12.9 223.4 %all-gather.11.cloned.1.call-start = ((), (), s32[]{:S(2)}) async-start(), calls=%async_computation.1 | async-start | bytes 10813440 | tf_op jit(solution)/shard_map/all_gather | solution.py:51
  271.3 13.3 %all-to-all-start = ((f32[4,32,256]{2,0,1:T(4,128)}), f32[4,32,256]{2,0,1:T(4,128)S(1)}, u32[]{:S(2)}, u32[]{:S(2)}) async-start(f32[4,32,256]{2,0,1:T(4,128)} %maximum_maximum_fusion), calls=%async_computation | async-start | bytes 262144 | tf_op jit(solution)/shard_map/all_to_all | solution.py:60
Sparse Core Ops, SparseCore 0:
  11.5 55.4 all-gather.12
  69.3 52.5 all-gather.14
  124.1 52.5 all-gather.16
  178.8 57.4 all-gather.10
where the time goes:
time: 307 us
  waiting for transfers between devices  198 us (64%)
  matrix products  43.3 us (14%)
  other arithmetic  19.3 us (6%)
  between operations  16.4 us (5%)
  blocking collectives  12.3 us (4%)
  local copies, waits for them, and re-layouts  12.1 us (4%)
  starting transfers between devices  5.6 us (2%)
    all_gather x4, waiting for transfers between devices, per_device(): block = lax.all_gather(piece, 'req', axis=0, tiled=False)  189 us
    dot_general x4, matrix products, chunk_stats(): logits = jnp.dot(block, matrix, preferred_element_type=jnp.float32)  43.3 us
    all_gather x1, blocking collectives, per_device(): everyone = lax.all_gather(own, 'tp', axis=0)  12.3 us
    reduce_sum x1, other arithmetic, chunk_stats(): weight_sum = jnp.sum(shifted, axis=-1)  12 us
    slice x1, local copies, waits for them, and re-layouts, per_device(): block = block[:, :step]  8.39 us
    all_to_all x1, waiting for transfers between devices, per_device(): lax.all_to_all(stats, 'req', split_axis=1, concat_axis=1, tiled=True)  7.21 us
  transfers between devices with their start and end apart: 5, of which 5 were waited for; matrix products, arithmetic and copies ran while one was open for 11% of the time, Pallas kernels for 0%

commit v1 on v0

--- a/solution.py
+++ b/solution.py
@@ -57,7 +57,10 @@
         st = chunk_stats(block.reshape(-1, block.shape[2]), target, head, own_vocab)
         parts.append(st.reshape(4, n_req, step))
     stats = jnp.concatenate(parts, axis=2)
-    arrived = lax.all_to_all(stats, "req", split_axis=1, concat_axis=1, tiled=True)
+    arrived = jnp.concatenate(
+        lax.all_to_all(jnp.stack(jnp.split(stats, lax.axis_size("req"), axis=1)), "req", 0, 0),
+        axis=1,
+    )
     own = merge(jnp.moveaxis(arrived, 1, 0), axis=0)
     own = jnp.stack(own)
     everyone = lax.all_gather(own, "tp", axis=0)

time: 307 us -> 325 us (1.059)
  local copies, waits for them, and re-layouts: 12.1 us -> 31 us
    unnamed x3 -> x34, local copies, waits for them, and re-layouts: 0.01 us -> 18.3 us
  transfers between devices with their start and end apart: 5 -> 5, of which waited for: 5 -> 5; matrix products, arithmetic and copies ran while one was open for 11% -> 10% of each run, Pallas kernels for 0% -> 0%
where the time goes in v1:
time: 325 us
  waiting for transfers between devices  198 us (61%)
  matrix products  43.3 us (13%)
  local copies, waits for them, and re-layouts  31 us (10%)
  other arithmetic  18.7 us (6%)
  between operations  16.4 us (5%)
  blocking collectives  12.3 us (4%)
  starting transfers between devices  5.6 us (2%)
    all_gather x4, waiting for transfers between devices, per_device(): block = lax.all_gather(piece, 'req', axis=0, tiled=False)  189 us
    dot_general x4, matrix products, chunk_stats(): logits = jnp.dot(block, matrix, preferred_element_type=jnp.float32)  43.3 us
    unnamed x34, local copies, waits for them, and re-layouts  18.3 us
    all_gather x1, blocking collectives, per_device(): everyone = lax.all_gather(own, 'tp', axis=0)  12.3 us
    reduce_sum x1, other arithmetic, chunk_stats(): weight_sum = jnp.sum(shifted, axis=-1)  12 us
    slice x1, local copies, waits for them, and re-layouts, per_device(): block = block[:, :step]  8.39 us
    all_to_all x1, waiting for transfers between devices, per_device(): lax.all_to_all(jnp.stack(jnp.split(stats, lax.axis_size('req'), axis=1)),...  7.21 us
  transfers between devices with their start and end apart: 5, of which 5 were waited for; matrix products, arithmetic and copies ran while one was open for 10% of the time, Pallas kernels for 0%

profile of v1, /device:TPU:0, one launch (start us, length us, event | category | flops | bytes accessed | tf_op | source)
XLA Modules:
  0.0 325.0 jit_solution(8526584782720007369)
XLA Ops:
  7.2 1.7 fusion.4
  8.9 1.5 fusion.6
  10.4 0.9 fusion.33
  11.4 0.7 all-gather.15.cloned.1.call-update
  12.2 0.7 all-gather.17.cloned.1.call-update
  12.9 0.7 fusion.29
  13.7 0.8 pad_maximum_fusion
  14.5 52.5 %all-gather.13.cloned.1.call-done = bf16[2048,2048]{1,0:T(8,128)(2,1)} async-done(((bf16[64,2048]{1,0:T(8,128)(2,1)}), bf16[2048,2048]{1,0:T(8,128)(2,1)}) %all-gather.13.cloned.1.call-update) | async-done | bytes 8388624 | tf_op jit(solution)/shard_map/all_gather | solution.py:51
  67.0 10.8 %fusion.38 = (f32[2048]{0:T(1024)S(1)}, f32[2048,768]{0,1:T(8,128)}) fusion(bf16[2048,2048]{1,0:T(8,128)(2,1)} %all-gather.13.cloned.1.call-done, bf16[2048,768]{1,0:T(8,128)(2,1)S(1)} %copy-done), kind=kOutput, calls=%fused_computation.156 | convolution fusion | flops 6444021760 | bytes 17833984 | tf_op jit(solution)/shard_map/dot_general | solution.py:10
  77.9 43.9 %all-gather.15.cloned.1.call-done = bf16[2048,2048]{1,0:T(8,128)(2,1)} async-done(((bf16[64,2048]{1,0:T(8,128)(2,1)}), bf16[2048,2048]{1,0:T(8,128)(2,1)}) %all-gather.15.cloned.1.call-update) | async-done | bytes 8388624 | tf_op jit(solution)/shard_map/all_gather | solution.py:51
  121.8 10.8 %fusion.39 = (f32[2048]{0:T(1024)S(1)}, f32[2048,768]{0,1:T(8,128)}) fusion(bf16[2048,2048]{1,0:T(8,128)(2,1)} %all-gather.15.cloned.1.call-done, bf16[2048,768]{1,0:T(8,128)(2,1)S(1)} %copy-done), kind=kOutput, calls=%fused_computation.157 | convolution fusion | flops 6444021760 | bytes 17833984 | tf_op jit(solution)/shard_map/dot_general | solution.py:10
  132.7 44.0 %all-gather.17.cloned.1.call-done = bf16[2048,2048]{1,0:T(8,128)(2,1)} async-done(((bf16[64,2048]{1,0:T(8,128)(2,1)}), bf16[2048,2048]{1,0:T(8,128)(2,1)}) %all-gather.17.cloned.1.call-update) | async-done | bytes 8388624 | tf_op jit(solution)/shard_map/all_gather | solution.py:51
  176.7 10.8 %fusion.40 = (f32[2048]{0:T(1024)S(1)}, f32[2048,768]{0,1:T(8,128)}) fusion(bf16[2048,2048]{1,0:T(8,128)(2,1)} %all-gather.17.cloned.1.call-done, bf16[2048,768]{1,0:T(8,128)(2,1)S(1)} %copy-done), kind=kOutput, calls=%fused_computation.158 | convolution fusion | flops 6444021760 | bytes 17833984 | tf_op jit(solution)/shard_map/dot_general | solution.py:10
  187.5 48.7 %all-gather.11.cloned.1.call-done = bf16[2560,2048]{1,0:T(8,128)(2,1)} async-done(((bf16[80,2048]{1,0:T(8,128)(2,1)}), bf16[2560,2048]{1,0:T(8,128)(2,1)}) %all-gather.11.cloned.1.call-update) | async-done | bytes 10485776 | tf_op jit(solution)/shard_map/all_gather | solution.py:51
  236.2 1.0 slice.104
  237.3 8.4 %slice.103 = bf16[32,64,2048]{2,1,0:T(8,128)(2,1)} slice(bf16[32,80,2048]{2,1,0:T(8,128)(2,1)} %bitcast.201), slice={[0:32], [0:64], [0:2048]} | slice | bytes 16777216 | tf_op jit(solution)/shard_map/slice | solution.py:55
  246.2 10.9 %fusion.37 = (f32[2048]{0:T(1024)S(1)}, f32[2048,768]{0,1:T(8,128)}) fusion(bf16[2048,2048]{1,0:T(8,128)(2,1)} %bitcast.199, bf16[2048,768]{1,0:T(8,128)(2,1)S(1)} %copy-done), kind=kOutput, calls=%fused_computation.155 | convolution fusion | flops 6444021760 | bytes 17833984 | tf_op jit(solution)/shard_map/dot_general | solution.py:10
  257.2 12.0 %fusion.3 = (f32[2048]{0:T(1024)S(1)}, f32[2048]{0:T(1024)S(1)}, f32[2048]{0:T(1024)S(1)}, f32[2048]{0:T(1024)S(1)}, f32[2048]{0:T(1024)S(1)}, /*index=5*/f32[20...) fusion(f32[2048,768]{0,1:T(8,128)} %get-tuple-element.71, ...), kind=kLoop, calls=%fused_computation.15 | loop fusion | flops 44015616 | bytes 25332736 | tf_op jit(solution)/shard_map/reduce_sum | solution.py:13
  270.6 0.6 constant_dynamic-update-slice_fusion.31
  271.2 0.6 constant_dynamic-update-slice_fusion.30
  274.2 0.6 constant_dynamic-update-slice_fusion.25
  276.5 0.6 constant_dynamic-update-slice_fusion.21
  278.3 0.6 constant_dynamic-update-slice_fusion.18
  281.3 0.6 constant_dynamic-update-slice_fusion.13
  281.9 0.6 constant_dynamic-update-slice_fusion.12
  283.1 0.6 constant_dynamic-update-slice_fusion.10
  284.8 0.6 constant_dynamic-update-slice_fusion.7
  286.0 0.6 constant_dynamic-update-slice_fusion.5
  289.6 5.4 %all-to-all-start = ((f32[32,4,1,256]{3,1,2,0:T(4,128)}), f32[32,4,1,256]{3,1,2,0:T(4,128)S(1)}, u32[]{:S(2)}, u32[]{:S(2)}) async-start(f32[32,4,1,256]{3,1,2,0:T(4,128)} %constant_dynamic-update-slice_fusion), calls=%async_computation | async-start | bytes 262144 | tf_op jit(solution)/shard_map/all_to_all | solution.py:61
  295.6 7.2 %all-to-all-done = f32[32,4,1,256]{3,1,2,0:T(4,128)S(1)} async-done(((f32[32,4,1,256]{3,1,2,0:T(4,128)}), f32[32,4,1,256]{3,1,2,0:T(4,128)S(1)}, u32[]{:S(2)}, u32[]{:S(2)}) %all-to-all-start) | async-done | bytes 131104 | tf_op jit(solution)/shard_map/all_to_all | solution.py:61
  303.0 12.3 %all-gather.5 = f32[4,4,256]{2,1,0:T(4,128)S(1)} all-gather(f32[1,4,256]{2,1,0:T(4,128)S(1)} %maximum_bitcast_fusion), channel_id=6, replica_groups=mesh['req'=32,'tp'=4] {'tp'}, dimensions={0}, use_global_device_ids=true | all-gather | bytes 20480 | tf_op jit(solution)/shard_map/all_gather | solution.py:66
  315.4 1.3 fusion.32
  (67 shorter events, 15.7 us)
Async XLA Ops:
  7.2 59.9 %copy-start = (bf16[2048,768]{1,0:T(8,128)(2,1)S(1)}, bf16[2048,768]{1,0:T(8,128)(2,1)}, u32[]{:S(2)}) copy-start(bf16[2048,768]{1,0:T(8,128)(2,1)} %param.9) | copy-start | bytes 9437188
  7.2 59.9 %all-gather.13.cloned.1.call-start = ((), (), s32[]{:S(2)}) async-start(), calls=%async_computation.2 | async-start | bytes 8650752 | tf_op jit(solution)/shard_map/all_gather | solution.py:51
  11.4 110.5 %all-gather.15.cloned.1.call-start = ((), (), s32[]{:S(2)}) async-start(), calls=%async_computation.3 | async-start | bytes 8650752 | tf_op jit(solution)/shard_map/all_gather | solution.py:51
  12.1 164.5 %all-gather.17.cloned.1.call-start = ((), (), s32[]{:S(2)}) async-start(), calls=%async_computation.4 | async-start | bytes 8650752 | tf_op jit(solution)/shard_map/all_gather | solution.py:51
  12.9 223.4 %all-gather.11.cloned.1.call-start = ((), (), s32[]{:S(2)}) async-start(), calls=%async_computation.1 | async-start | bytes 10813440 | tf_op jit(solution)/shard_map/all_gather | solution.py:51
  289.6 13.3 %all-to-all-start = ((f32[32,4,1,256]{3,1,2,0:T(4,128)}), f32[32,4,1,256]{3,1,2,0:T(4,128)S(1)}, u32[]{:S(2)}, u32[]{:S(2)}) async-start(f32[32,4,1,256]{3,1,2,0:T(4,128)} %constant_dynamic-update-slice_fusion), calls=%async_computation | async-start | bytes 262144 | tf_op jit(solution)/shard_map/all_to_all | solution.py:61
Sparse Core Ops, SparseCore 0:
  11.5 55.4 all-gather.12
  69.3 52.5 all-gather.14
  124.1 52.5 all-gather.16
  178.8 57.4 all-gather.10
